TPU v7x, 128 devices: a whole 4x4x4 slice. The times are simulated.
128 devices in a mesh: freq: 2 (over core), vs: 64 (over z, y, x).
Axes of the slice: x: 4, y: 4, z: 4, core: 2. Of those that a mesh axis runs over, the one named last changes fastest.
Arguments:
- kernel: bfloat16 [4, 2, 256, 16384], P('freq', None, None, 'vs'), may hold values from -0.03125 to 0.03125
- sources: bfloat16 [4, 2, 2048, 16384], P('freq', None, 'vs'), may hold values from -6 to 6
- observed: float32 [256, 160, 2048], P('freq', None, 'vs'), may hold values from -6 to 6
- gate_start: int32 [256], P('freq'), may hold values from 0 to 80, as said below
- gate_length: int32 [256], P('freq'), may hold values from 1 to 160
Outputs:
- gradient: bfloat16 [4, 2, 2048, 16384], P('freq', None, 'vs')
- misfit: float32 [256, 160, 2048], P('freq', None, 'vs')
Inputs may be any that keep to these rules, and one draw needn't show every extreme that they name: gate_start + gate_length <= 160 for every receiver.
All inputs are finite; a program needn't handle non-finite values.
Results may differ from a plain program's by a relative error of at most 0.0057.
Values may be sent and summed in bfloat16 or wider, within the bound.
No kernel may reach another device: no remote copies, remote signals or barrier semaphores. Data moves between devices by JAX's collectives and lax.ppermute only.
A program may use at most 128 MiB of HBM per device.

v0:
```python
import jax
import jax.numpy as jnp
from jax import lax
from jax.sharding import PartitionSpec as P

NS = 16384
RW = 256


def complex_apply(kern, model):
    form = "frs,fvs->frv"
    real_part = jnp.einsum(
        form, kern[:, 0], model[:, 0], preferred_element_type=jnp.float32
    ) - jnp.einsum(form, kern[:, 1], model[:, 1], preferred_element_type=jnp.float32)
    imag_part = jnp.einsum(
        form, kern[:, 0], model[:, 1], preferred_element_type=jnp.float32
    ) + jnp.einsum(form, kern[:, 1], model[:, 0], preferred_element_type=jnp.float32)
    return jnp.stack([real_part, imag_part], 1)


def complex_adjoint(kern, spectrum):
    form = "frv,frs->fvs"
    real_part = jnp.einsum(
        form, spectrum[:, 0], kern[:, 0], preferred_element_type=jnp.float32
    ) + jnp.einsum(form, spectrum[:, 1], kern[:, 1], preferred_element_type=jnp.float32)
    imag_part = jnp.einsum(
        form, spectrum[:, 1], kern[:, 0], preferred_element_type=jnp.float32
    ) - jnp.einsum(form, spectrum[:, 0], kern[:, 1], preferred_element_type=jnp.float32)
    factor = (NS / RW) ** 0.5
    return factor * jnp.stack([real_part, imag_part], 1)


def transform_tables(count, samples):
    sample_index = jnp.arange(samples, dtype=jnp.int32)
    bin_index = samples // 4 + jnp.arange(count, dtype=jnp.int32)
    phase = sample_index[:, None] * bin_index[None, :] % samples
    theta = 2.0 * jnp.pi / samples * phase.astype(jnp.float32)
    return (jnp.cos(theta), jnp.sin(theta))


def local(kernel, sources, observed, gate_start, gate_length):
    gathered = lax.all_gather(kernel, "vs", axis=3, tiled=True)
    forward = complex_apply(gathered, sources)
    field = forward.astype(jnp.bfloat16)
    timed = lax.all_to_all(field, "freq", split_axis=2, concat_axis=0, tiled=True)
    count = timed.shape[0]
    samples = observed.shape[1]
    cosine, sine = transform_tables(count, samples)
    scale = count ** (-0.5)
    values = timed.astype(jnp.float32)
    highest = lax.Precision.HIGHEST
    signal = scale * (
        jnp.einsum("tf,frv->rtv", cosine, values[:, 0], precision=highest)
        - jnp.einsum("tf,frv->rtv", sine, values[:, 1], precision=highest)
    )
    sample_index = jnp.arange(samples, dtype=jnp.int32)
    inside = (sample_index[None, :] >= gate_start[:, None]) & (
        sample_index[None, :] < (gate_start + gate_length)[:, None]
    )
    gate_mask = inside.astype(jnp.float32)
    misfit = gate_mask[:, :, None] * (signal - observed)
    back_real = scale * jnp.einsum("tf,rtv->frv", cosine, misfit, precision=highest)
    back_imag = -scale * jnp.einsum("tf,rtv->frv", sine, misfit, precision=highest)
    back_spectrum = jnp.stack([back_real, back_imag], 1).astype(jnp.bfloat16)
    spectral = lax.all_to_all(back_spectrum, "freq", split_axis=0, concat_axis=2, tiled=True)
    gradient = complex_adjoint(gathered, spectral).astype(jnp.bfloat16)
    return (gradient, misfit)


def solution(mesh):
    return jax.shard_map(
        local,
        mesh=mesh,
        in_specs=(
            P("freq", None, None, "vs"),
            P("freq", None, "vs", None),
            P("freq", None, "vs"),
            P("freq"),
            P("freq"),
        ),
        out_specs=(P("freq", None, "vs", None), P("freq", None, "vs")),
        check_vma=False,
    )
```

profile of v0, /device:TPU:1, one launch (start us, length us, event | category | flops | bytes accessed | tf_op | source)
XLA Modules:
  0.0 335.3 jit_solution(14792505252984407137)
XLA Ops:
  7.2 1.9 copy.15
  9.1 0.7 add.36
  9.8 0.7 fusion.41
  10.5 229.3 %all-gather.2.cloned.1.call-done = bf16[2,2,256,16384]{3,2,0,1:T(8,128)(2,1)} async-done(((bf16[2,2,256,256]{3,2,0,1:T(8,128)(2,1)}), bf16[2,2,256,16384]{3,2,0,1:T(8,128)(2,1)}) %all-gather.2.cloned.1.call-update) | async-done | bytes 33554448 | tf_op jit(solution)/shard_map/all_gather | solution.py:42
  239.8 10.0 %fusion.4 = f32[2,256,32]{1,2,0:T(8,128)S(1)} fusion(bf16[2,2,256,16384]{3,2,0,1:T(8,128)(2,1)} %all-gather.2.cloned.1.call-done, bf16[2,2,32,16384]{3,2,1,0:T(8,128)(2,1)} %param.6), kind=kOutput, calls=%fused_computation.8 | convolution fusion | flops 536870912 | bytes 18939904 | tf_op jit(solution)/shard_map/frs,fvs->frv/dot_general | solution.py:15
  249.7 8.6 %fusion.5 = f32[2,256,32]{1,2,0:T(8,128)S(1)} fusion(bf16[2,2,256,16384]{3,2,0,1:T(8,128)(2,1)} %all-gather.2.cloned.1.call-done, bf16[2,2,32,16384]{3,2,1,0:T(8,128)(2,1)S(1)} %copy-done.1), kind=kOutput, calls=%fused_computation.9 | convolution fusion | flops 536870912 | bytes 18939904 | tf_op jit(solution)/shard_map/frs,fvs->frv/dot_general | solution.py:12
  258.4 8.6 %fusion.37 = bf16[2,1,256,32]{2,3,0,1:T(8,128)(2,1)S(1)} fusion(f32[2,256,32]{1,2,0:T(8,128)S(1)} %fusion.4, bf16[2,2,32,16384]{3,2,1,0:T(8,128)(2,1)S(1)} %copy-done.1, bf16[2,2,256,16384]{3,2,0,1:T(8,128)(2,1)} %all-gather.2.cloned.1.call-done), kind=kOutput, calls=%fused_computation.35 | convolution fusion | flops 536903680 | bytes 18972672 | tf_op jit(solution)/shard_map/frs,fvs->frv/dot_general | solution.py:17
  267.0 8.6 %fusion.34 = bf16[2,1,256,32]{2,3,0,1:T(8,128)(2,1)S(1)} fusion(f32[2,256,32]{1,2,0:T(8,128)S(1)} %fusion.5, bf16[2,2,32,16384]{3,2,1,0:T(8,128)(2,1)S(1)} %copy-done.1, bf16[2,2,256,16384]{3,2,0,1:T(8,128)(2,1)} %all-gather.2.cloned.1.call-done), kind=kOutput, calls=%fused_computation.34 | convolution fusion | flops 536903680 | bytes 18972672 | tf_op jit(solution)/shard_map/frs,fvs->frv/dot_general | solution.py:14
  275.7 0.2 copy.18
  275.9 0.3 reshape.54
  276.2 5.6 %all_to_all.36 = bf16[2,2,8192]{2,1,0:T(2,128)(2,1)S(1)} all-to-all(bf16[2,2,8192]{2,1,0:T(2,128)(2,1)S(1)} %reshape.54), channel_id=1, replica_groups=mesh['freq'=2,'vs'=64] {'freq'}, dimensions={0} | all-to-all | bytes 131072 | tf_op jit(solution)/shard_map/all_to_all | solution.py:45
  281.8 0.2 reshape.55
  282.1 1.3 fusion.42
  283.5 3.0 fusion.9
  286.5 1.4 fusion.32
  287.9 1.4 fusion.33
  289.3 3.0 copy.24
  292.4 3.8 %all_to_all.37 = bf16[4,2,128,32]{2,3,1,0:T(8,128)(2,1)S(1)} all-to-all(bf16[4,2,128,32]{2,3,1,0:T(8,128)(2,1)S(1)} %copy.21), channel_id=1, replica_groups=mesh['freq'=2,'vs'=64] {'freq'}, dimensions={0} | all-to-all | bytes 131072 | tf_op jit(solution)/shard_map/all_to_all | solution.py:65
  296.4 7.3 %fusion.2 = f32[2,32,16384]{2,1,0:T(8,128)S(1)} fusion(bf16[2,2,256,16384]{3,2,0,1:T(8,128)(2,1)} %all-gather.2.cloned.1.call-done, bf16[2,2,256,32]{2,3,0,1:T(8,128)(2,1)S(1)} %all_to_all.33), kind=kOutput, calls=%fused_computation.6 | convolution fusion | flops 536870912 | bytes 21004288 | tf_op jit(solution)/shard_map/frv,frs->fvs/dot_general | solution.py:26
  303.7 7.3 %fusion.3 = f32[2,32,16384]{2,1,0:T(8,128)S(1)} fusion(bf16[2,2,256,16384]{3,2,0,1:T(8,128)(2,1)} %all-gather.2.cloned.1.call-done, bf16[2,2,256,32]{2,3,0,1:T(8,128)(2,1)S(1)} %all_to_all.33), kind=kOutput, calls=%fused_computation.7 | convolution fusion | flops 536870912 | bytes 21004288 | tf_op jit(solution)/shard_map/frv,frs->fvs/dot_general | solution.py:23
  311.0 7.3 %fusion.1 = f32[2,1,32,16384]{3,2,0,1:T(8,128)S(1)} fusion(f32[2,32,16384]{2,1,0:T(8,128)S(1)} %fusion.2, bf16[2,2,256,16384]{3,2,0,1:T(8,128)(2,1)} %all-gather.2.cloned.1.call-done, bf16[2,2,256,32]{2,3,0,1:T(8,128)(2,1)S(1)} %all_to_all.33), kind=kOutput, calls=%fused_computation.3 | convolution fusion | flops 537919488 | bytes 25198592 | tf_op jit(solution)/shard_map/frv,frs->fvs/dot_general | solution.py:28
  318.3 7.3 %fusion = f32[2,1,32,16384]{3,2,0,1:T(8,128)S(1)} fusion(f32[2,32,16384]{2,1,0:T(8,128)S(1)} %fusion.3, bf16[2,2,256,16384]{3,2,0,1:T(8,128)(2,1)} %all-gather.2.cloned.1.call-done, bf16[2,2,256,32]{2,3,0,1:T(8,128)(2,1)S(1)} %all_to_all.33), kind=kOutput, calls=%fused_computation.2 | convolution fusion | flops 537919488 | bytes 25198592 | tf_op jit(solution)/shard_map/frv,frs->fvs/dot_general | solution.py:25
  325.7 0.5 fusion.8
  326.2 2.3 copy.23
  (13 shorter events, 0.4 us)
Async XLA Ops:
  7.2 232.6 %all-gather.2.cloned.1.call-start = ((), (), s32[]{:S(2)}) async-start(), calls=%async_computation.2 | async-start | bytes 34078720 | tf_op jit(solution)/shard_map/all_gather | solution.py:42
  239.8 10.0 %copy-start.1 = (bf16[2,2,32,16384]{3,2,1,0:T(8,128)(2,1)S(1)}, bf16[2,2,32,16384]{3,2,1,0:T(8,128)(2,1)}, u32[]{:S(2)}) copy-start(bf16[2,2,32,16384]{3,2,1,0:T(8,128)(2,1)} %param.6) | copy-start | bytes 12582916
  275.7 7.8 %copy-start = (f32[128,160,32]{0,2,1:T(8,128)S(1)}, f32[128,160,32]{0,2,1:T(8,128)}, u32[]{:S(2)}) copy-start(f32[128,160,32]{0,2,1:T(8,128)} %param.7) | copy-start | bytes 7864324
Sparse Core Ops, SparseCore 0:
  11.2 228.4 all-gather.1
where the time goes:
time: 336 us; the launch traced here: 335 us
  waiting for transfers between devices  229 us (68%)
  matrix products  72.3 us (22%)
  between operations  14.2 us (4%)
  blocking collectives  9.47 us (3%)
  local copies, waits for them, and re-layouts  8.13 us (2%)
    all_gather x1, waiting for transfers between devices, local(): gathered = lax.all_gather(kernel, 'vs', axis=3, tiled=True)  229 us
    dot_general x1, matrix products, complex_apply(): jnp.einsum(form, kern[:, 0], model[:, 1], preferred_element_type=jnp.floa...  9.96 us
    dot_general x1, matrix products, complex_apply(): jnp.einsum(form, kern[:, 1], model[:, 0], preferred_element_type=jnp.floa...  8.64 us
    dot_general x1, matrix products, complex_apply(): jnp.einsum(form, kern[:, 1], model[:, 1], preferred_element_type=jnp.floa...  8.64 us
    dot_general x1, matrix products, complex_apply(): jnp.einsum(form, kern[:, 0], model[:, 0], preferred_element_type=jnp.floa...  8.62 us
    unnamed x9, local copies, waits for them, and re-layouts  7.7 us
    dot_general x1, matrix products, complex_adjoint(): jnp.einsum(form, spectrum[:, 0], kern[:, 1], preferred_element_type=jnp.f...  7.33 us
    dot_general x1, matrix products, complex_adjoint(): jnp.einsum(form, spectrum[:, 1], kern[:, 1], preferred_element_type=jnp.f...  7.33 us
  transfers between devices with their start and end apart: 1, of which 1 were waited for; matrix products, arithmetic and copies ran while one was open for 0% of the time, Pallas kernels for 0%

commit v1 on v0

--- a/solution.py
+++ b/solution.py
@@ -39,7 +39,8 @@
 
 
 def local(kernel, sources, observed, gate_start, gate_length):
-    gathered = lax.all_gather(kernel, "vs", axis=3, tiled=True)
+    copies = jnp.concatenate([kernel] * lax.axis_size("vs"), axis=3)
+    gathered = lax.all_to_all(copies, "vs", 3, 3, tiled=True)
     forward = complex_apply(gathered, sources)
     field = forward.astype(jnp.bfloat16)
     timed = lax.all_to_all(field, "freq", split_axis=2, concat_axis=0, tiled=True)

time: 336 us -> 959 us (2.85)
  the two profiles are of different devices: /device:TPU:1 before, /device:TPU:99 now
where the time goes in v1:
time: 959 us; the launch traced here: 948 us
  waiting for transfers between devices  645 us (67%)
  local copies, waits for them, and re-layouts  203 us (21%)
  matrix products  76.4 us (8%)
  starting transfers between devices  10.1 us (1%)
    all_to_all x1, waiting for transfers between devices, local(): gathered = lax.all_to_all(copies, 'vs', 3, 3, tiled=True)  645 us
    unnamed x88, local copies, waits for them, and re-layouts  176 us
    slice x1, local copies, waits for them, and re-layouts, complex_apply(): kern[:, 1]  26.1 us
  transfers between devices with their start and end apart: 1, of which 1 were waited for; matrix products, arithmetic and copies ran while one was open for 0% of the time, Pallas kernels for 0%

profile of v1, /device:TPU:99, one launch (start us, length us, event | category | flops | bytes accessed | tf_op | source)
XLA Modules:
  0.0 947.8 jit_solution(7560903681050962613)
XLA Ops:
  0.6 1.4 copy.78
  38.1 1.4 constant_dynamic-update-slice_fusion.32
  74.4 13.7 %constant_dynamic-update-slice_fusion.1 = bf16[2,2,256,16384]{2,0,1,3:T(2,128)(2,1)} fusion(bf16[2,2,256,16384]{2,0,1,3:T(2,128)(2,1)} %constant_dynamic-update-slice_fusion.2, bf16[2,2,256,256]{2,0,1,3:T(2,128)(2,1)S(1)} %copy.78), kind=kLoop, calls=%fused_computation.43 | loop fusion | bytes 1048576
  89.3 10.1 %all-to-all-start = ((bf16[2,2,256,16384]{2,0,1,3:T(2,128)(2,1)}), bf16[2,2,256,16384]{2,0,1,3:T(2,128)(2,1)}, u32[]{:S(2)}, u32[]{:S(2)}) async-start(bf16[2,2,256,16384]{2,0,1,3:T(2,128)(2,1)} %constant_dynamic-update-slice_fusion), calls=%async_computation | async-start | bytes 67108864 | tf_op jit(solution)/shard_map/all_to_all | solution.py:43
  99.5 645.0 %all-to-all-done = bf16[2,2,256,16384]{2,0,1,3:T(2,128)(2,1)} async-done(((bf16[2,2,256,16384]{2,0,1,3:T(2,128)(2,1)}), bf16[2,2,256,16384]{2,0,1,3:T(2,128)(2,1)}, u32[]{:S(2)}, u32[]{:S(2)}) %all-to-all-start) | async-done | bytes 33554464 | tf_op jit(solution)/shard_map/all_to_all | solution.py:43
  744.6 26.1 %fusion.90 = (bf16[2,1,256,16384]{2,0,1,3:T(2,128)(2,1)}, bf16[2,1,256,16384]{2,0,1,3:T(2,128)(2,1)}) fusion(bf16[2,2,256,16384]{2,0,1,3:T(2,128)(2,1)} %all-to-all-done), kind=kLoop, calls=%fused_computation.144 | loop fusion | bytes 67108864 | tf_op jit(solution)/shard_map/slice | solution.py:14
  770.6 41.0 %copy.155 = bf16[2,1,256,16384]{3,2,0,1:T(8,128)(2,1)} copy(bf16[2,1,256,16384]{2,0,1,3:T(2,128)(2,1)} %get-tuple-element.6) | data formatting | bytes 33554432
  811.6 9.8 %fusion.6 = f32[2,256,32]{1,2,0:T(8,128)S(1)} fusion(bf16[2,1,256,16384]{3,2,0,1:T(8,128)(2,1)} %copy.155, bf16[2,2,32,16384]{3,2,1,0:T(8,128)(2,1)} %param.6), kind=kOutput, calls=%fused_computation.8 | convolution fusion | flops 536870912 | bytes 18939904 | tf_op jit(solution)/shard_map/frs,fvs->frv/dot_general | solution.py:14
  821.5 9.8 %fusion.4 = f32[2,256,32]{1,2,0:T(8,128)S(1)} fusion(bf16[2,1,256,16384]{3,2,0,1:T(8,128)(2,1)} %copy.155, bf16[2,2,32,16384]{3,2,1,0:T(8,128)(2,1)} %param.6), kind=kOutput, calls=%fused_computation.6 | convolution fusion | flops 536870912 | bytes 18939904 | tf_op jit(solution)/shard_map/frs,fvs->frv/dot_general | solution.py:17
  831.3 41.1 %copy.153 = bf16[2,1,256,16384]{3,2,0,1:T(8,128)(2,1)} copy(bf16[2,1,256,16384]{2,0,1,3:T(2,128)(2,1)} %get-tuple-element.7) | data formatting | bytes 33554432
  872.4 8.9 fusion.50
  881.4 8.9 fusion.55
  890.8 5.3 all_to_all.41
  897.8 2.9 fusion.17
  900.7 1.4 fusion.49
  902.2 1.4 fusion.48
  903.7 4.0 all_to_all.42
  907.8 8.9 fusion.10
  916.7 8.9 fusion.8
  925.6 3.0 copy.152
  928.7 10.9 %fusion = f32[2,1,32,16384]{3,2,0,1:T(8,128)} fusion(f32[2,32,16384]{2,1,0:T(8,128)S(1)} %fusion.10, bf16[2,1,256,16384]{3,2,0,1:T(8,128)(2,1)} %copy.155, bf16[2,2,256,32]{2,3,0,1:T(8,128)(2,1)S(1)} %all_to_all.37), kind=kOutput, calls=%fused_computation.2 | convolution fusion | flops 537919488 | bytes 25198592 | tf_op jit(solution)/shard_map/frv,frs->fvs/dot_general | solution.py:25
  939.6 3.0 fusion.1
  942.6 2.5 fusion.16
  945.1 2.3 copy.151
  (94 shorter events, 74.6 us)
Async XLA Ops:
  89.3 10.1 %copy-start.3 = (s32[128]{0:T(128)S(1)}, s32[128]{0:T(128)}, u32[]{:S(2)}) copy-start(s32[128]{0:T(128)} %param.8) | copy-start | bytes 1540
  89.3 10.1 %copy-start.4 = (s32[128]{0:T(128)S(1)}, s32[128]{0:T(128)}, u32[]{:S(2)}) copy-start(s32[128]{0:T(128)} %param.9) | copy-start | bytes 1540
  89.3 655.2 %all-to-all-start = ((bf16[2,2,256,16384]{2,0,1,3:T(2,128)(2,1)}), bf16[2,2,256,16384]{2,0,1,3:T(2,128)(2,1)}, u32[]{:S(2)}, u32[]{:S(2)}) async-start(bf16[2,2,256,16384]{2,0,1,3:T(2,128)(2,1)} %constant_dynamic-update-slice_fusion), calls=%async_computation | async-start | bytes 67108864 | tf_op jit(solution)/shard_map/all_to_all | solution.py:43
  831.3 66.5 %copy-start.2 = (f32[128,160,32]{0,2,1:T(8,128)S(1)}, f32[128,160,32]{0,2,1:T(8,128)}, u32[]{:S(2)}) copy-start(f32[128,160,32]{0,2,1:T(8,128)} %param.7) | copy-start | bytes 7864324
  900.7 1.5 copy-start
  907.8 17.8 %copy-start.1 = (f32[128,160,32]{0,1,2:T(8,128)S(1)}, f32[128,160,32]{0,1,2:T(8,128)}, u32[]{:S(2)}) copy-start(f32[128,160,32]{0,1,2:T(8,128)} %copy-done) | copy-start | bytes 7864324
  916.7 22.9 %slice-start = ((s8[16777216]{0:T(1024)(128)(4,1)}), s8[4194304]{0:T(1024)(128)(4,1)S(1)}, s32[]{:S(2)}) async-start(s8[16777216]{0:T(1024)(128)(4,1)} %bitcast.110), calls=%async_computation.3 | async-start | bytes 8388608
  916.7 22.9 %slice-start.1 = ((s8[16777216]{0:T(1024)(128)(4,1)}), s8[4194304]{0:T(1024)(128)(4,1)S(1)}, s32[]{:S(2)}) async-start(s8[16777216]{0:T(1024)(128)(4,1)} %bitcast.110), calls=%async_computation.4 | async-start | bytes 8388608
  925.6 14.0 %slice-start.2 = ((s8[16777216]{0:T(1024)(128)(4,1)}), s8[4194304]{0:T(1024)(128)(4,1)S(1)}, s32[]{:S(2)}) async-start(s8[16777216]{0:T(1024)(128)(4,1)} %bitcast.110), calls=%async_computation.5 | async-start | bytes 8388608
  928.7 10.9 %slice-start.3 = ((s8[16777216]{0:T(1024)(128)(4,1)}), s8[4194304]{0:T(1024)(128)(4,1)S(1)}, s32[]{:S(2)}) async-start(s8[16777216]{0:T(1024)(128)(4,1)} %bitcast.110), calls=%async_computation.6 | async-start | bytes 8388608
